TPU v7x, 256 devices: a whole 4x4x8 slice. The times are simulated.
256 devices in a mesh: ctx: 32 (over x_lo, z, core), head: 8 (over x_hi, y).
Axes of the slice: x: 4 (x_hi: 2, x_lo: 2; x = x_hi * 2 + x_lo), y: 4, z: 8, core: 2. Of those that a mesh axis runs over, the one named last changes fastest.
Arguments:
- tokens: bfloat16 [8192, 3072], P('ctx', 'head'), may hold values from -48 to 48
- block_order: int32 [64], replicated, may hold values from 0 to 63, each once
- block_mask: int32 [64, 64], replicated, may hold values from 0 to 1, as said below
- w_query: bfloat16 [3072, 3072], P(None, 'head'), may hold values from -0.109375 to 0.109375
- w_key: bfloat16 [3072, 3072], P(None, 'head'), may hold values from -0.109375 to 0.109375
- w_value: bfloat16 [3072, 3072], P(None, 'head'), may hold values from -0.109375 to 0.109375
- w_out: bfloat16 [3072, 3072], P('head'), may hold values from -0.109375 to 0.109375
Outputs:
- mixed: bfloat16 [8192, 3072], P('ctx', 'head')
Inputs may be any that keep to these rules, and one draw needn't show every extreme that they name: `block_order`: a permutation of the block numbers. block_mask[f, f] = 1 for every block f.
All inputs are finite; a program needn't handle non-finite values.
Results may differ from a plain program's by a relative error of at most 0.02.
The roundings to bfloat16 on the way count: a program that leaves them out, or rounds other values in their place, can miss the bound.
Values may be sent and summed in bfloat16 or wider, within the bound.
A program may use at most 128 MiB of HBM per device.

v0:
```python
import jax
import jax.numpy as jnp
from jax import lax
from jax.sharding import PartitionSpec as P

HEAD_DIM = 128
BLOCK = 128


def per_device(tokens, block_order, block_mask, w_query, w_key, w_value, w_out):
    row_count = tokens.shape[0]
    local_width = w_query.shape[1]
    local_heads = local_width // HEAD_DIM
    block_count = block_order.shape[0]
    portion = lax.all_gather(tokens, "head", axis=1, tiled=True)
    projected = tuple(
        (
            jnp.dot(portion, weight, preferred_element_type=jnp.float32)
            for weight in (w_query, w_key, w_value)
        )
    )
    query_rows, key_rows, value_rows = [
        part_sum.astype(jnp.bfloat16).reshape(row_count, local_heads, HEAD_DIM)
        for part_sum in projected
    ]
    frame_ids = jnp.arange(block_count, dtype=jnp.int32)
    placed = (block_order[None, :] == frame_ids[:, None]).astype(jnp.float32)
    mask_float = block_mask.astype(jnp.float32)
    cycle_live = jnp.dot(
        jnp.dot(placed.T, mask_float, precision=lax.Precision.HIGHEST),
        placed,
        precision=lax.Precision.HIGHEST,
    )
    cycle_index = lax.axis_index("ctx")
    global_rows = cycle_index * row_count + jnp.arange(row_count, dtype=jnp.int32)
    row_blocks = global_rows // BLOCK
    row_pick = (row_blocks[:, None] == frame_ids[None, :]).astype(jnp.float32)
    live_columns = jnp.dot(row_pick, cycle_live, precision=lax.Precision.HIGHEST).T
    inv_root = 1.0 / HEAD_DIM**0.5

    def update(state, key_tile, value_tile, key_keep):
        top_now, total_now, accum = state
        scores = (
            jnp.einsum("qhd,khd->hqk", query_rows, key_tile, preferred_element_type=jnp.float32)
            * inv_root
        )
        allowed = key_keep[None, :, None]
        top_next = jnp.maximum(top_now, jnp.max(jnp.where(allowed, scores, -1e30), axis=-1))
        factor = jnp.exp(top_now - top_next)
        weights = jnp.where(allowed, jnp.exp(scores - top_next[..., None]), 0.0)
        total_next = total_now * factor + jnp.sum(weights, axis=-1)
        accum = accum * factor[..., None] + jnp.einsum(
            "hqk,khd->hqd",
            weights.astype(jnp.bfloat16),
            value_tile,
            preferred_element_type=jnp.float32,
        )
        return (top_next, total_next, accum)

    initial = (
        jnp.full((local_heads, row_count), -1e30, jnp.float32),
        jnp.zeros((local_heads, row_count), jnp.float32),
        jnp.zeros((local_heads, row_count, HEAD_DIM), jnp.float32),
    )
    carry = initial
    key_part = lax.all_gather(key_rows, "ctx", axis=0, tiled=True)
    value_part = lax.all_gather(value_rows, "ctx", axis=0, tiled=True)
    tile_count = key_part.shape[0] // BLOCK
    key_tiles = key_part.reshape(tile_count, BLOCK, local_heads, HEAD_DIM)
    value_tiles = value_part.reshape(tile_count, BLOCK, local_heads, HEAD_DIM)

    def advance(state, inputs):
        key_tile, value_tile, offset = inputs
        key_keep = lax.dynamic_index_in_dim(live_columns, offset, 0, keepdims=False) > 0.5
        state = update(state, key_tile, value_tile, key_keep)
        return (state, None)

    carry, _ = lax.scan(
        advance, carry, (key_tiles, value_tiles, jnp.arange(tile_count, dtype=jnp.int32))
    )
    top_final, total_final, accum_final = carry
    attended = (
        (accum_final / total_final[..., None])
        .transpose(1, 0, 2)
        .reshape(row_count, local_width)
        .astype(jnp.bfloat16)
    )
    partial_out = jnp.dot(attended, w_out, preferred_element_type=jnp.float32)
    return lax.psum_scatter(
        partial_out.astype(jnp.bfloat16), "head", scatter_dimension=1, tiled=True
    )


def solution(mesh):
    in_specs = (
        P("ctx", "head"),
        P(),
        P(),
        P(None, "head"),
        P(None, "head"),
        P(None, "head"),
        P("head", None),
    )
    out_specs = P("ctx", "head")
    return jax.shard_map(
        per_device, mesh=mesh, in_specs=in_specs, out_specs=out_specs, check_vma=False
    )
```

profile of v0, /device:TPU:32, one launch (start us, length us, event | category | flops | bytes accessed | tf_op | source)
XLA Modules:
  0.0 652.0 jit_solution(12298507190897239615)
XLA Ops:
  7.3 59.7 %all-gather.4.cloned.1.call-done = bf16[256,3072]{1,0:T(8,128)(2,1)} async-done(((bf16[256,384]{1,0:T(8,128)(2,1)}), bf16[256,3072]{1,0:T(8,128)(2,1)}) %all-gather.4.cloned.1.call-update) | async-done | bytes 1572880 | tf_op jit(solution)/shard_map/all_gather | solution.py:15
  67.0 3.1 convolution_convert_fusion.1
  71.1 3.1 convolution_convert_fusion.3
  75.8 3.1 convolution_convert_fusion.2
  79.3 69.0 %all-gather.8.cloned.1.call-done = bf16[8192,3,128]{0,2,1:T(8,128)(2,1)} async-done(((bf16[256,3,128]{0,2,1:T(8,128)(2,1)}), bf16[8192,3,128]{0,2,1:T(8,128)(2,1)}) %all-gather.8.cloned.1.call-update) | async-done | bytes 6291472 | tf_op jit(solution)/shard_map/all_gather | solution.py:67
  148.3 8.6 %copy.25 = bf16[8192,3,128]{2,0,1:T(8,128)(2,1)} copy(bf16[8192,3,128]{0,2,1:T(8,128)(2,1)} %all-gather.8.cloned.1.call-done) | data formatting | bytes 12582912 | tf_op jit(solution)/shard_map/all_gather | solution.py:67
  156.9 71.3 %all-gather.6.cloned.1.call-done = bf16[8192,3,128]{0,2,1:T(8,128)(2,1)} async-done(((bf16[256,3,128]{0,2,1:T(8,128)(2,1)}), bf16[8192,3,128]{0,2,1:T(8,128)(2,1)}) %all-gather.6.cloned.1.call-update) | async-done | bytes 6291472 | tf_op jit(solution)/shard_map/all_gather | solution.py:66
  228.2 8.6 %copy.22 = bf16[8192,3,128]{2,0,1:T(8,128)(2,1)} copy(bf16[8192,3,128]{0,2,1:T(8,128)(2,1)} %all-gather.6.cloned.1.call-done) | data formatting | bytes 12582912 | tf_op jit(solution)/shard_map/all_gather | solution.py:66
  236.8 323.9 %while.15 = (s32[]{:T(128)}, f32[3,256]{1,0:T(4,128)S(1)}, f32[3,256]{1,0:T(4,128)S(1)}, f32[3,256,128]{2,1,0:T(8,128)S(1)}, s32[64]{0:T(128)S(1)}, /*index=5*/f...) while((s32[]{:T(128)}, f32[3,256]{1,0:T(4,128)S(1)}, ...), condition=%wide.region_3.4_spmd.clone, body=%wide.region_0.3_spmd.clone.sunk | while | flops 51515396 | bytes 2410691 | solution.py:78
  250.7 1.2 convolution_add_fusion.2
  260.8 1.2 convolution_add_fusion.2
  265.9 1.2 convolution_add_fusion.2
  276.0 1.2 convolution_add_fusion.2
  281.1 1.2 convolution_add_fusion.2
  291.2 1.2 convolution_add_fusion.2
  301.3 1.2 convolution_add_fusion.2
  306.4 1.2 convolution_add_fusion.2
  316.5 1.2 convolution_add_fusion.2
  321.6 1.2 convolution_add_fusion.2
  331.7 1.2 convolution_add_fusion.2
  341.8 1.2 convolution_add_fusion.2
  346.9 1.2 convolution_add_fusion.2
  357.0 1.2 convolution_add_fusion.2
  362.1 1.2 convolution_add_fusion.2
  372.2 1.2 convolution_add_fusion.2
  377.2 1.2 convolution_add_fusion.2
  387.4 1.2 convolution_add_fusion.2
  397.5 1.2 convolution_add_fusion.2
  560.9 2.2 convolution_convert_fusion
  563.1 2.6 copy.31
  565.7 78.1 %reduce-scatter.4.cloned.1.call-done = bf16[384,256]{1,0:T(8,128)(2,1)} async-done(((bf16[3072,256]{1,0:T(8,128)(2,1)}), bf16[384,256]{1,0:T(8,128)(2,1)}) %reduce-scatter.4.cloned.1.call-update) | async-done | bytes 196624
  643.8 1.7 copy.32
  (521 shorter events, 177.1 us)
Async XLA Ops:
  6.5 554.4 %copy-start = (bf16[384,3072]{1,0:T(8,128)(2,1)S(1)}, bf16[384,3072]{1,0:T(8,128)(2,1)}, u32[]{:S(2)}) copy-start(bf16[384,3072]{1,0:T(8,128)(2,1)} %param.15) | copy-start | bytes 7077892
  6.5 60.5 %all-gather.4.cloned.1.call-start = ((), (), s32[]{:S(2)}) async-start(), calls=%async_computation.1 | async-start | bytes 1769472 | tf_op jit(solution)/shard_map/all_gather | solution.py:15
  7.3 141.0 %all-gather.8.cloned.1.call-start = ((), (), s32[]{:S(2)}) async-start(), calls=%async_computation.3 | async-start | bytes 6488064 | tf_op jit(solution)/shard_map/all_gather | solution.py:67
  71.0 4.2 copy-start.1
  71.0 4.2 copy-start.2
  71.0 157.2 %all-gather.6.cloned.1.call-start = ((), (), s32[]{:S(2)}) async-start(), calls=%async_computation.2 | async-start | bytes 6488064 | tf_op jit(solution)/shard_map/all_gather | solution.py:66
  75.0 568.7 %reduce-scatter.4.cloned.1.call-start = ((), (), s32[]{:S(2)}) async-start(), calls=%async_computation.4 | async-start | bytes 1769472
Sparse Core Ops, SparseCore 0:
  9.8 57.1 all-gather.3
  71.1 77.1 all-gather.7
  150.1 78.0 all-gather.5
  565.8 77.9 reduce-scatter.3
where the time goes:
time: 658 us; the launch traced here: 652 us
  waiting for transfers between devices  279 us (42%)
  matrix products  162 us (25%)
  loops' own time  127 us (19%)
  local copies, waits for them, and re-layouts  61.4 us (9%)
  between operations  13.3 us (2%)
  other arithmetic  8.91 us (1%)
    another operation x1, loops' own time, per_device(): lax.scan(advance, carry, (key_tiles, value_tiles, jnp.arange(tile_count,...  127 us
    unnamed x5, waiting for transfers between devices  78.9 us
    dot_general x64, matrix products, update(): jnp.einsum('hqk,khd->hqd', weights.astype(jnp.bfloat16), value_tile, pref...  77.5 us
    dot_general x64, matrix products, update(): jnp.einsum('qhd,khd->hqk', query_rows, key_tile, preferred_element_type=j...  72.4 us
    all_gather x1, waiting for transfers between devices, per_device(): key_part = lax.all_gather(key_rows, 'ctx', axis=0, tiled=True)  71.3 us
    all_gather x1, waiting for transfers between devices, per_device(): value_part = lax.all_gather(value_rows, 'ctx', axis=0, tiled=True)  69 us
    all_gather x1, waiting for transfers between devices, per_device(): portion = lax.all_gather(tokens, 'head', axis=1, tiled=True)  59.7 us
    dynamic_slice x64, local copies, waits for them, and re-layouts, per_device(): lax.scan(advance, carry, (key_tiles, value_tiles, jnp.arange(tile_count,...  37.5 us
  transfers between devices with their start and end apart: 4, of which 4 were waited for; matrix products, arithmetic and copies ran while one was open for 3% of the time, Pallas kernels for 0%

commit v1 on v0

--- a/solution.py
+++ b/solution.py
@@ -12,7 +12,9 @@
     local_width = w_query.shape[1]
     local_heads = local_width // HEAD_DIM
     block_count = block_order.shape[0]
-    portion = lax.all_gather(tokens, "head", axis=1, tiled=True)
+    portion = jnp.concatenate(
+        lax.all_to_all(jnp.stack([tokens] * lax.axis_size("head")), "head", 0, 0), axis=1
+    )
     projected = tuple(
         (
             jnp.dot(portion, weight, preferred_element_type=jnp.float32)

time: 658 us -> 628 us (0.954)
  waiting for transfers between devices: 279 us -> 219 us
  blocking collectives: 0 us -> 29.6 us
    all_gather x1 -> x0, waiting for transfers between devices: 59.7 us -> none  [per_device(): portion = lax.all_gather(tokens, 'head', axis=1, tiled=True)]
    all_to_all x0 -> x1, blocking collectives: none -> 29.6 us  [per_device(): lax.all_to_all(jnp.stack([tokens] * lax.axis_size('head')), 'head', 0, 0)]
    unnamed x5 -> x4, waiting for transfers between devices: 78.9 us -> 78.2 us
  transfers between devices with their start and end apart: 4 -> 3, of which waited for: 4 -> 3; matrix products, arithmetic and copies ran while one was open for 3% -> 3% of each run, Pallas kernels for 0% -> 0%
where the time goes in v1:
time: 628 us; the launch traced here: 622 us
  waiting for transfers between devices  219 us (35%)
  matrix products  160 us (25%)
  loops' own time  127 us (20%)
  local copies, waits for them, and re-layouts  63.9 us (10%)
  blocking collectives  29.6 us (5%)
  between operations  13.3 us (2%)
  other arithmetic  8.91 us (1%)
    another operation x1, loops' own time, per_device(): lax.scan(advance, carry, (key_tiles, value_tiles, jnp.arange(tile_count,...  127 us
    unnamed x4, waiting for transfers between devices  78.2 us
    dot_general x64, matrix products, update(): jnp.einsum('hqk,khd->hqd', weights.astype(jnp.bfloat16), value_tile, pref...  77.5 us
    dot_general x64, matrix products, update(): jnp.einsum('qhd,khd->hqk', query_rows, key_tile, preferred_element_type=j...  72.4 us
    all_gather x1, waiting for transfers between devices, per_device(): key_part = lax.all_gather(key_rows, 'ctx', axis=0, tiled=True)  71.2 us
    all_gather x1, waiting for transfers between devices, per_device(): value_part = lax.all_gather(value_rows, 'ctx', axis=0, tiled=True)  69.6 us
    dynamic_slice x64, local copies, waits for them, and re-layouts, per_device(): lax.scan(advance, carry, (key_tiles, value_tiles, jnp.arange(tile_count,...  37.5 us
    all_to_all x1, blocking collectives, per_device(): lax.all_to_all(jnp.stack([tokens] * lax.axis_size('head')), 'head', 0, 0)  29.6 us
  transfers between devices with their start and end apart: 3, of which 3 were waited for; matrix products, arithmetic and copies ran while one was open for 3% of the time, Pallas kernels for 0%

profile of v1, /device:TPU:32, one launch (start us, length us, event | category | flops | bytes accessed | tf_op | source)
XLA Modules:
  0.0 622.2 jit_solution(4880684858560692670)
XLA Ops:
  7.9 29.6 %all_to_all.5 = bf16[8,256,384]{1,2,0:T(8,128)(2,1)S(1)} all-to-all(bf16[8,256,384]{1,2,0:T(8,128)(2,1)S(1)} %stack.2), channel_id=1, replica_groups=mesh['ctx'=32,'head'=8] {'head'}, dimensions={0} | all-to-all | bytes 3145728 | tf_op jit(solution)/shard_map/all_to_all | solution.py:16
  40.6 3.2 convolution_convert_fusion.3
  45.4 3.2 convolution_convert_fusion.2
  48.9 69.6 %all-gather.5.cloned.1.call-done = bf16[8192,3,128]{0,2,1:T(8,128)(2,1)} async-done(((bf16[256,3,128]{0,2,1:T(8,128)(2,1)}), bf16[8192,3,128]{0,2,1:T(8,128)(2,1)}) %all-gather.5.cloned.1.call-update) | async-done | bytes 6291472 | tf_op jit(solution)/shard_map/all_gather | solution.py:69
  118.5 8.6 %copy.27 = bf16[8192,3,128]{2,0,1:T(8,128)(2,1)} copy(bf16[8192,3,128]{0,2,1:T(8,128)(2,1)} %all-gather.5.cloned.1.call-done) | data formatting | bytes 12582912 | tf_op jit(solution)/shard_map/all_gather | solution.py:69
  127.1 71.2 %all-gather.3.cloned.1.call-done = bf16[8192,3,128]{0,2,1:T(8,128)(2,1)} async-done(((bf16[256,3,128]{0,2,1:T(8,128)(2,1)}), bf16[8192,3,128]{0,2,1:T(8,128)(2,1)}) %all-gather.3.cloned.1.call-update) | async-done | bytes 6291472 | tf_op jit(solution)/shard_map/all_gather | solution.py:68
  198.3 8.6 %copy.24 = bf16[8192,3,128]{2,0,1:T(8,128)(2,1)} copy(bf16[8192,3,128]{0,2,1:T(8,128)(2,1)} %all-gather.3.cloned.1.call-done) | data formatting | bytes 12582912 | tf_op jit(solution)/shard_map/all_gather | solution.py:68
  206.9 323.9 %while.15 = (s32[]{:T(128)}, f32[3,256]{1,0:T(4,128)S(1)}, f32[3,256]{1,0:T(4,128)S(1)}, f32[3,256,128]{2,1,0:T(8,128)S(1)}, s32[64]{0:T(128)S(1)}, /*index=5*/f...) while((s32[]{:T(128)}, f32[3,256]{1,0:T(4,128)S(1)}, ...), condition=%wide.region_3.4_spmd.clone, body=%wide.region_0.3_spmd.clone.sunk | while | flops 51515396 | bytes 2410691 | solution.py:80
  215.8 1.2 convolution_add_fusion.2
  220.8 1.2 convolution_add_fusion.2
  225.9 1.2 convolution_add_fusion.2
  236.0 1.2 convolution_add_fusion.2
  246.1 1.2 convolution_add_fusion.2
  251.2 1.2 convolution_add_fusion.2
  261.3 1.2 convolution_add_fusion.2
  266.4 1.2 convolution_add_fusion.2
  276.5 1.2 convolution_add_fusion.2
  281.6 1.2 convolution_add_fusion.2
  291.7 1.2 convolution_add_fusion.2
  301.8 1.2 convolution_add_fusion.2
  306.9 1.2 convolution_add_fusion.2
  317.0 1.2 convolution_add_fusion.2
  322.1 1.2 convolution_add_fusion.2
  332.2 1.2 convolution_add_fusion.2
  342.3 1.2 convolution_add_fusion.2
  347.4 1.2 convolution_add_fusion.2
  357.5 1.2 convolution_add_fusion.2
  362.5 1.2 convolution_add_fusion.2
  531.0 2.2 convolution_convert_fusion
  533.2 2.6 copy.33
  535.8 78.1 %reduce-scatter.4.cloned.1.call-done = bf16[384,256]{1,0:T(8,128)(2,1)} async-done(((bf16[3072,256]{1,0:T(8,128)(2,1)}), bf16[384,256]{1,0:T(8,128)(2,1)}) %reduce-scatter.4.cloned.1.call-update) | async-done | bytes 196624
  613.9 1.7 copy.34
  (525 shorter events, 178.7 us)
Async XLA Ops:
  6.5 524.5 %copy-start = (bf16[384,3072]{1,0:T(8,128)(2,1)S(1)}, bf16[384,3072]{1,0:T(8,128)(2,1)}, u32[]{:S(2)}) copy-start(bf16[384,3072]{1,0:T(8,128)(2,1)} %param.15) | copy-start | bytes 7077892
  6.5 111.9 %all-gather.5.cloned.1.call-start = ((), (), s32[]{:S(2)}) async-start(), calls=%async_computation.3 | async-start | bytes 6488064 | tf_op jit(solution)/shard_map/all_gather | solution.py:69
  7.8 30.9 %copy-start.4 = (bf16[3072,384]{1,0:T(8,128)(2,1)S(1)}, bf16[3072,384]{1,0:T(8,128)(2,1)}, u32[]{:S(2)}) copy-start(bf16[3072,384]{1,0:T(8,128)(2,1)} %param.14) | copy-start | bytes 7077892
  37.5 1.2 copy-start.1
  40.5 4.2 copy-start.2
  40.5 4.2 copy-start.3
  40.6 157.7 %all-gather.3.cloned.1.call-start = ((), (), s32[]{:S(2)}) async-start(), calls=%async_computation.2 | async-start | bytes 6488064 | tf_op jit(solution)/shard_map/all_gather | solution.py:68
  44.6 569.3 %reduce-scatter.4.cloned.1.call-start = ((), (), s32[]{:S(2)}) async-start(), calls=%async_computation.4 | async-start | bytes 1769472
Sparse Core Ops, SparseCore 0:
  40.7 77.7 all-gather.4
  120.2 77.9 all-gather.2
  535.9 77.9 reduce-scatter.3
